TPU v7x, 256 devices: a whole 4x4x8 slice. The times are simulated.
256 devices in a mesh: rollout: 2 (over core), context: 32 (over z, x), head: 4 (over y).
Axes of the slice: x: 4, y: 4, z: 8, core: 2. Of those that a mesh axis runs over, the one named last changes fastest.
Arguments:
- inner_raw: bfloat16 [16384, 8192], P(('rollout', 'context', 'head')), parts along dimension 0, may hold values from -6 to 6
- pairs_raw: bfloat16 [16384, 8, 2, 128], P(('rollout', 'context', 'head')), parts along dimension 0, may hold values from -2.5 to 2.5
- gate_raw: bfloat16 [16384, 8192], P(('rollout', 'context'), 'head'), parts along dimension 0, may hold values from -6 to 6
- step_raw: bfloat16 [16384, 128], P(('rollout', 'context'), 'head'), parts along dimension 0, may hold values from -3 to 3
- step_bias: float32 [128], P('head'), may hold values from -0.5 to 0.5
- rate_log: float32 [128], P('head'), may hold values from -13.5 to -2.8, as said below
- skip_gain: float32 [128], P('head'), may hold values from 0.5 to 2
- conv_inner: float32 [5, 8192], replicated, may hold values from -2.5 to 2.5
- conv_pairs: float32 [5, 8, 2, 128], replicated, may hold values from -2.5 to 2.5
- norm_gain: float32 [8192], P('head'), may hold values from 0.5 to 1.5
Outputs:
- mixer_out: bfloat16 [16384, 8192], P(('rollout', 'context', 'head')), parts along dimension 0
There are 2 independent parts, one for each index of `rollout`. A program takes and returns all parts, laid end to end along the dimension named above; an argument that names none is the same for every part. Nothing has to cross between parts.
Inputs may be any that keep to these rules, and one draw needn't show every extreme that they name: `rate_log`: one value a head.
All inputs are finite; a program needn't handle non-finite values.
Results may differ from a plain program's by a relative error of at most 0.012.
The roundings to bfloat16 on the way count: a program that leaves them out, or rounds other values in their place, can miss the bound.
Values may be sent and summed in bfloat16 or wider, within the bound.
No kernel may reach another device: no remote copies, remote signals or barrier semaphores. Data moves between devices by JAX's collectives and lax.ppermute only.
A program may use at most 128 MiB of HBM per device.

v0:
```python
import jax
import jax.numpy as jnp
from jax import lax
from jax.sharding import PartitionSpec as P

BLOCK = 256


def from_behind(block, axis, distance):
    devices = range(lax.axis_size(axis))
    route = [(i - distance, i) for i in devices if i - distance in devices]
    return lax.ppermute(block, axis, route)


def prefix(part, axis, combine, identity):
    place = lax.axis_index(axis)
    gathered = jax.tree.map(lambda a: lax.all_gather(a, axis), part)
    state = jax.tree.map(lambda a, e: jnp.zeros_like(a) + jnp.asarray(e, a.dtype), part, identity)

    def one(lap, state):
        return combine(
            state, jax.tree.map(lambda a: lax.dynamic_index_in_dim(a, lap, 0, False), gathered)
        )

    return lax.fori_loop(0, place, one, state)


def convolve(raw_rows, before, weight):
    tap_count = weight.shape[0] - 1
    row_count = raw_rows.shape[0]
    extended = jnp.concatenate([before, raw_rows], axis=0).astype(jnp.float32)
    summed = weight[tap_count][None, :] + weight[0][None, :] * extended[0:row_count]
    for offset in range(1, tap_count):
        summed = summed + weight[offset][None, :] * extended[offset : offset + row_count]
    return jax.nn.silu(summed).astype(jnp.bfloat16)


def block_intra(inner_conv, pairs_conv, step_size, log_cum, groups):
    block_len, head_count = step_size.shape
    per_group = head_count // groups
    head_width = inner_conv.shape[1] // head_count
    pair_view = pairs_conv.reshape(block_len, groups, 2, -1)
    scores = jnp.einsum(
        "ign,jgn->gij", pair_view[:, :, 1], pair_view[:, :, 0], preferred_element_type=jnp.float32
    )
    lower_tri = lax.broadcasted_iota(jnp.int32, (block_len, block_len), 0) >= lax.broadcasted_iota(
        jnp.int32, (block_len, block_len), 1
    )
    cum_t = log_cum.T
    log_gap = jnp.minimum(cum_t[:, :, None] - cum_t[:, None, :], 0.0)
    decay_mat = jnp.where(lower_tri[None], jnp.exp(log_gap), 0.0) * step_size.T[:, None, :]
    weights = (scores[:, None] * decay_mat.reshape(groups, per_group, block_len, block_len)).astype(
        jnp.bfloat16
    )
    inner_view = inner_conv.reshape(block_len, groups, per_group, head_width)
    intra_out = jnp.einsum(
        "gkij,jgkp->igkp", weights, inner_view, preferred_element_type=jnp.float32
    )
    return intra_out.reshape(block_len, head_count * head_width)


def block_state(inner_conv, pairs_conv, step_size, log_cum, groups):
    block_len, head_count = step_size.shape
    per_group = head_count // groups
    head_width = inner_conv.shape[1] // head_count
    tail_w = jnp.exp(log_cum[-1][None, :] - log_cum) * step_size
    weighted = (
        inner_conv.reshape(block_len, head_count, head_width).astype(jnp.float32)
        * tail_w[:, :, None]
    ).astype(jnp.bfloat16)
    weighted = weighted.reshape(block_len, groups, per_group, head_width)
    bmat = pairs_conv.reshape(block_len, groups, 2, -1)[:, :, 0]
    local_state = jnp.einsum("jgn,jgkp->gknp", bmat, weighted, preferred_element_type=jnp.float32)
    return (local_state.reshape(head_count, -1, head_width), jnp.exp(log_cum[-1]))


def finish(
    inner_conv, pairs_conv, gate_rows, intra_out, carry_state, log_cum, skip_gain, norm_gain, groups
):
    block_len, head_count = log_cum.shape
    per_group = head_count // groups
    head_width = inner_conv.shape[1] // head_count
    cmat = pairs_conv.reshape(block_len, groups, 2, -1)[:, :, 1]
    held = carry_state.astype(jnp.bfloat16).reshape(groups, per_group, -1, head_width)
    carried = jnp.einsum("ign,gknp->igkp", cmat, held, preferred_element_type=jnp.float32)
    carried = carried.reshape(block_len, head_count, head_width) * jnp.exp(log_cum)[:, :, None]
    mixed = (
        intra_out
        + carried.reshape(block_len, -1)
        + jnp.repeat(skip_gain, head_width)[None, :] * inner_conv.astype(jnp.float32)
    )
    gated_out = mixed * jax.nn.silu(gate_rows.astype(jnp.float32))
    grouped = gated_out.reshape(block_len, groups, -1)
    inv_rms = lax.rsqrt(jnp.mean(grouped * grouped, axis=2, keepdims=True) + 1e-05)
    return ((grouped * inv_rms).reshape(block_len, -1) * norm_gain[None, :]).astype(jnp.bfloat16)


def chain_combine(earlier, later):
    return (earlier[0] * later[0], later[0][:, None, None] * earlier[1] + later[1])


def absorb(running, element):
    local_state, block_decay = element
    return (block_decay[:, None, None] * running + local_state, None)


def on_device(
    inner_raw,
    pairs_raw,
    gate_raw,
    step_raw,
    step_bias,
    rate_log,
    skip_gain,
    conv_inner,
    conv_pairs,
    norm_gain,
):
    shards = lax.axis_size("head")
    row_count = inner_raw.shape[0]
    tap_count = conv_inner.shape[0] - 1
    inner_full = inner_raw.shape[1]
    pairs_flat = pairs_raw.reshape(row_count, -1)
    conv_flat = conv_pairs.reshape(tap_count + 1, -1)
    width_local = gate_raw.shape[1]
    head_local = step_raw.shape[1]
    groups_local = pairs_raw.shape[1] // shards
    last_rows = jnp.concatenate(
        [inner_raw[row_count - tap_count :], pairs_flat[row_count - tap_count :]], axis=1
    )
    before = from_behind(last_rows, ("context", "head"), 1)
    outgoing_inner = convolve(inner_raw, before[:, :inner_full], conv_inner)
    outgoing_pairs = convolve(pairs_flat, before[:, inner_full:], conv_flat)
    got_inner, got_pairs = (
        lax.all_to_all(outgoing_inner, "head", split_axis=1, concat_axis=0, tiled=True),
        lax.all_to_all(outgoing_pairs, "head", split_axis=1, concat_axis=0, tiled=True),
    )
    length = got_inner.shape[0]
    block_count = length // BLOCK
    step_size = jax.nn.softplus(step_raw.astype(jnp.float32) + step_bias[None, :])
    log_steps = (-jnp.exp(rate_log)[None, :] * step_size).reshape(block_count, BLOCK, head_local)
    lower_tri = (
        lax.broadcasted_iota(jnp.int32, (BLOCK, BLOCK), 0)
        >= lax.broadcasted_iota(jnp.int32, (BLOCK, BLOCK), 1)
    ).astype(jnp.float32)
    log_cum = jnp.einsum("ij,cjh->cih", lower_tri, log_steps, precision=lax.Precision.HIGHEST)
    step_blocks = step_size.reshape(block_count, BLOCK, head_local)
    inner_blocks = got_inner.reshape(block_count, BLOCK, -1)
    pair_blocks = got_pairs.reshape(block_count, BLOCK, -1)
    gate_blocks = gate_raw.reshape(block_count, BLOCK, -1)
    inputs = (inner_blocks, pair_blocks, step_blocks, log_cum)

    def intra_part(element):
        return block_intra(element[0], element[1], element[2], element[3], groups_local)

    def state_part(element):
        return block_state(element[0], element[1], element[2], element[3], groups_local)

    def both_parts(element):
        local_state, block_decay = state_part(element)
        return (intra_part(element), local_state, block_decay)

    intra_all, states, decays = lax.map(both_parts, inputs)
    start_zero = jnp.zeros(states.shape[1:], jnp.float32)
    device_state, _ = lax.scan(absorb, start_zero, (states, decays))
    device_decay = jnp.prod(decays, axis=0)
    incoming = prefix(
        (device_decay, device_state),
        "context",
        chain_combine,
        (jnp.ones_like(device_decay), jnp.zeros_like(device_state)),
    )

    def emit(carry_state, element):
        inner_rows, pair_rows, gate_rows, intra_out, cum_rows, local_state, block_decay = element
        result = finish(
            inner_rows,
            pair_rows,
            gate_rows,
            intra_out,
            carry_state,
            cum_rows,
            skip_gain,
            norm_gain,
            groups_local,
        )
        return (block_decay[:, None, None] * carry_state + local_state, result)

    _, results = lax.scan(
        emit,
        incoming[1],
        (inner_blocks, pair_blocks, gate_blocks, intra_all, log_cum, states, decays),
    )
    head_rows = results.reshape(length, width_local)
    return lax.all_to_all(head_rows, "head", split_axis=0, concat_axis=1, tiled=True)


def solution(mesh):
    placed = (
        P(("rollout", "context", "head"), None),
        P(("rollout", "context", "head"), None, None, None),
        P(("rollout", "context"), "head"),
        P(("rollout", "context"), "head"),
        P("head"),
        P("head"),
        P("head"),
        P(),
        P(),
        P("head"),
    )
    return jax.shard_map(
        on_device,
        mesh=mesh,
        in_specs=placed,
        out_specs=P(("rollout", "context", "head"), None),
        check_vma=False,
    )
```

profile of v0, /device:TPU:230, one launch (start us, length us, event | category | flops | bytes accessed | tf_op | source)
XLA Modules:
  0.0 496.4 jit_solution(1473578907943598542)
XLA Ops:
  8.3 3.5 collective-permute-start
  13.3 1.7 fusion.49
  19.2 4.2 all-to-all-start.1
  26.1 4.0 all-to-all-done.1
  30.0 3.5 all-to-all-start
  36.2 11.0 %all-to-all-done = bf16[64,4,2048]{2,0,1:T(8,128)(2,1)S(1)} async-done(((bf16[64,4,2048]{2,0,1:T(8,128)(2,1)}), bf16[64,4,2048]{2,0,1:T(8,128)(2,1)S(1)}, u32[]{:S(2)}, u32[]{:S(2)}) %all-to-all-start) | async-done | bytes 1048608 | tf_op jit(solution)/shard_map/all_to_all | solution.py:135
  47.2 2.2 reshape.197
  49.4 2.5 copy.90
  51.9 1.7 fusion.23
  58.4 38.2 %all-gather = f32[32,1,32]{2,1,0:T(1,128)} all-gather(f32[1,1,32]{2,1,0:T(1,128)S(1)} %get-tuple-element.157), channel_id=2, replica_groups=mesh['rollout'=2,'context'=32,'head'=4] {'context'}, dimensions={0}, use_global_device_ids=true | all-gather | bytes 4224 | tf_op jit(solution)/shard_map/all_gather | solution.py:17
  98.6 1.8 copy.97
  100.4 5.3 %fusion = f32[2,16,64,256]{3,2,1,0:T(8,128)} fusion(bf16[256,2,16,64]{0,3,2,1:T(8,128)(2,1)S(1)} %copy-done.1, f32[2,16,256]{2,1,0:T(8,128)S(1)} %bitcast.138, f32[2,16,256]{2,1,0:T(8,128)S(1)} %bitcast.136, f32[2,256,256]{2,1,0:T(8,128)} %fusion.35, pred[256,256]{1,0:T(8,128)(4,1)S(1)} %copy-done.11), kind=kOutput, calls=%fused_computation.4 | convolution fusion | flops 281018368 | bytes 3801088 | tf_op jit(solution)/shard_map/while/body/eval_jaxpr/gkij,jgkp->igkp/dot_general | solution.py:56
  105.7 177.0 %all-gather.3.cloned.1.call-done = f32[32,32,128,64]{2,3,1,0:T(8,128)} async-done(((f32[1,32,128,64]{2,3,1,0:T(8,128)}), f32[32,32,128,64]{2,3,1,0:T(8,128)}) %all-gather.3.cloned.1.call-update) | async-done | bytes 33554448 | tf_op jit(solution)/shard_map/all_gather | solution.py:17
  284.2 178.0 %while.3 = (s32[]{:T(128)}, f32[32,128,64]{2,1,0:T(8,128)}, s32[]{:T(128)}, f32[32,32]{1,0:T(8,128)}, f32[32,32,128,64]{2,3,1,0:T(8,128)}, /*index=5*/s32[]{:T(128)}, s32[]{:T(128)}, s32[]{:T(128)}) while((s32[]{:T(128)}, f32[32,128,64]{2,1,0:T(8,128)}, s32[]{:T(128)}, f32[32,32]{1,0:T(8,128)}, f32[32,32,128,64]{2,3,1,0:T(8,128)}, ...), condition=%wide.region_1.2_spmd, body=%wide.region_0.1_spmd.sunk | while | flops 524293 | bytes 7340551 | solution.py:25
  286.8 3.2 bitcast_add_fusion.3
  292.6 3.2 bitcast_add_fusion.3
  298.3 3.2 bitcast_add_fusion.3
  304.1 3.2 bitcast_add_fusion.3
  309.8 3.2 bitcast_add_fusion.3
  315.6 3.2 bitcast_add_fusion.3
  321.3 3.2 bitcast_add_fusion.3
  327.1 3.2 bitcast_add_fusion.3
  332.8 3.2 bitcast_add_fusion.3
  338.5 3.2 bitcast_add_fusion.3
  344.3 3.2 bitcast_add_fusion.3
  350.0 3.2 bitcast_add_fusion.3
  355.8 3.2 bitcast_add_fusion.3
  361.5 3.2 bitcast_add_fusion.3
  367.2 3.2 bitcast_add_fusion.3
  373.0 3.2 bitcast_add_fusion.3
  378.7 3.2 bitcast_add_fusion.3
  384.5 3.2 bitcast_add_fusion.3
  390.2 3.2 bitcast_add_fusion.3
  396.0 3.2 bitcast_add_fusion.3
  401.7 3.2 bitcast_add_fusion.3
  407.5 3.2 bitcast_add_fusion.3
  413.2 3.2 bitcast_add_fusion.3
  418.9 3.2 bitcast_add_fusion.3
  424.7 3.2 bitcast_add_fusion.3
  430.4 3.2 bitcast_add_fusion.3
  436.2 3.2 bitcast_add_fusion.3
  441.9 3.2 bitcast_add_fusion.3
  447.6 3.2 bitcast_add_fusion.3
  453.4 3.2 bitcast_add_fusion.3
  459.1 3.2 bitcast_add_fusion.3
  462.3 1.9 convert_element_type.68
  464.5 3.1 fusion.11
  469.7 18.8 %all_to_all.51 = bf16[4,64,2048]{2,1,0:T(8,128)(2,1)S(1)} all-to-all(bf16[4,64,2048]{2,1,0:T(8,128)(2,1)S(1)} %bitcast.118), channel_id=1, replica_groups=mesh['rollout'=2,'context'=32,'head'=4] {'head'}, dimensions={0} | all-to-all | bytes 2097152 | tf_op jit(solution)/shard_map/all_to_all | solution.py:195
  (175 shorter events, 104.2 us)
Async XLA Ops:
  8.3 9.7 %collective-permute-start = (bf16[4,10240]{1,0:T(4,128)(2,1)S(1)}, bf16[4,10240]{1,0:T(4,128)(2,1)S(1)}, u32[]{:S(2)}, u32[]{:S(2)}) collective-permute-start(bf16[4,10240]{1,0:T(4,128)(2,1)S(1)} %pad_maximum_fusion), channel_id=1, source_target_pairs={{0,1},{1,2},{2,3},{3,4},{4,5},{5,6},{6,7},{7,8},{8,9},{9,10},{10,1... | collective-permute-start | bytes 245768 | tf_op jit(solution)/shard_map/ppermute | solution.py:12
  16.0 2.0 copy-start.12
  18.0 5.4 %copy-start.5 = (bf16[64,8192]{1,0:T(8,128)(2,1)S(1)}, bf16[64,8192]{1,0:T(8,128)(2,1)}, u32[]{:S(2)}) copy-start(bf16[64,8192]{1,0:T(8,128)(2,1)} %param.12) | copy-start | bytes 3145732
  19.2 10.8 %all-to-all-start.1 = ((bf16[64,4,512]{2,0,1:T(8,128)(2,1)}), bf16[64,4,512]{2,0,1:T(8,128)(2,1)S(1)}, u32[]{:S(2)}, u32[]{:S(2)}) async-start(bf16[64,4,512]{2,0,1:T(8,128)(2,1)} %bitcast.111), calls=%async_computation.1 | async-start | bytes 524288 | tf_op jit(solution)/shard_map/all_to_all | solution.py:136
  25.0 8.6 %copy-start.17 = (f32[32]{0:T(128)S(1)}, f32[32]{0:T(128)}, u32[]{:S(2)}) copy-start(f32[32]{0:T(128)} %param.16) | copy-start | bytes 388
  30.0 17.2 %all-to-all-start = ((bf16[64,4,2048]{2,0,1:T(8,128)(2,1)}), bf16[64,4,2048]{2,0,1:T(8,128)(2,1)S(1)}, u32[]{:S(2)}, u32[]{:S(2)}) async-start(bf16[64,4,2048]{2,0,1:T(8,128)(2,1)} %bitcast.110), calls=%async_computation | async-start | bytes 2097152 | tf_op jit(solution)/shard_map/all_to_all | solution.py:135
  33.6 249.1 %all-gather.3.cloned.1.call-start = ((), (), s32[]{:S(2)}) async-start(), calls=%async_computation.3 | async-start | bytes 34603008 | tf_op jit(solution)/shard_map/all_gather | solution.py:17
  53.6 1.2 copy-start.18
  53.6 2.1 copy-start.9
  53.6 2.8 copy-start.8
  53.6 3.5 copy-start.6
  54.7 42.5 %copy-start.7 = (bf16[256,2,1,128]{3,2,1,0:T(2,128)(2,1)S(1)}, bf16[256,2,1,128]{3,2,1,0:T(2,128)(2,1)}, u32[]{:S(2)}) copy-start(bf16[256,2,1,128]{3,2,1,0:T(2,128)(2,1)} %get-tuple-element.147) | copy-start | bytes 393220
  98.5 1.9 copy-start.1
  98.5 1.8 copy-start.11
  98.5 1.8 copy-start.13
  98.6 1.8 copy-start.15
  462.3 1.9 copy-start.2
  462.3 2.2 copy-start.3
  462.3 2.2 copy-start.14
  464.4 3.2 copy-start
  464.4 3.2 copy-start.4
  464.4 3.2 copy-start.10
  464.4 3.2 copy-start.16
Sparse Core Ops, SparseCore 0:
  54.9 227.7 all-gather.2
where the time goes:
time: 500 us; the launch traced here: 496 us
  waiting for transfers between devices  192 us (38%)
  other arithmetic  107 us (21%)
  local copies, waits for them, and re-layouts  103 us (21%)
  blocking collectives  57 us (11%)
  between operations  13.8 us (3%)
  matrix products  12.1 us (2%)
  starting transfers between devices  11.2 us (2%)
    all_gather x1, waiting for transfers between devices, prefix(): gathered = jax.tree.map(lambda a: lax.all_gather(a, axis), part)  177 us
    add x31, other arithmetic, chain_combine(): later[0][:, None, None] * earlier[1] + later[1]  97.7 us
    dynamic_slice x62, local copies, waits for them, and re-layouts, one(): lax.dynamic_index_in_dim(a, lap, 0, False)  58.8 us
    all_gather x1, blocking collectives, prefix(): gathered = jax.tree.map(lambda a: lax.all_gather(a, axis), part)  38.2 us
    mul x31, local copies, waits for them, and re-layouts, chain_combine(): later[0][:, None, None] * earlier[1] + later[1]  21.1 us
    all_to_all x1, blocking collectives, on_device(): lax.all_to_all(head_rows, 'head', split_axis=0, concat_axis=1, tiled=True)  18.8 us
    all_to_all x1, waiting for transfers between devices, on_device(): lax.all_to_all(outgoing_inner, 'head', split_axis=1, concat_axis=0, tiled...  11 us
  transfers between devices with their start and end apart: 4, of which 3 were waited for; matrix products, arithmetic and copies ran while one was open for 5% of the time, Pallas kernels for 0%

commit v1 on v0

--- a/solution.py
+++ b/solution.py
@@ -131,8 +131,33 @@
     before = from_behind(last_rows, ("context", "head"), 1)
     outgoing_inner = convolve(inner_raw, before[:, :inner_full], conv_inner)
     outgoing_pairs = convolve(pairs_flat, before[:, inner_full:], conv_flat)
+
+    def hold_spans_in(sample, dim_k, dim_i=0):
+        met_up = lax.axis_index("head")
+        w2 = lax.axis_size("head")
+        all_rows, formed = (w2, met_up)
+        prior = list(sample.shape)
+        block_next = sample.shape[dim_k] // all_rows
+        prior[dim_k] = block_next
+        small = prior[dim_i]
+        prior[dim_i] = small * all_rows
+        mat_out = jnp.zeros(prior, sample.dtype)
+        for d in [*range(all_rows)]:
+            outer = lax.dynamic_slice_in_dim(
+                sample, (formed ^ d) * block_next, block_next, axis=dim_k
+            )
+            if d:
+                pieces_in = []
+                for ii in tuple(range(all_rows)):
+                    pieces_in.append((ii, ii ^ d))
+                outer = lax.ppermute(outer, "head", pieces_in)
+            mat_out = lax.dynamic_update_slice_in_dim(
+                mat_out, outer, (formed ^ d) * small, axis=dim_i
+            )
+        return mat_out
+
     got_inner, got_pairs = (
-        lax.all_to_all(outgoing_inner, "head", split_axis=1, concat_axis=0, tiled=True),
+        hold_spans_in(outgoing_inner, 1),
         lax.all_to_all(outgoing_pairs, "head", split_axis=1, concat_axis=0, tiled=True),
     )
     length = got_inner.shape[0]

time: 500 us -> 509 us (1.018)
  other arithmetic: 107 us -> 120 us
  waiting for transfers between devices: 192 us -> 203 us
  local copies, waits for them, and re-layouts: 103 us -> 95.5 us
  matrix products: 12.1 us -> 6.4 us
    mul x31, local copies, waits for them, and re-layouts: 21.1 us -> 0.38 us  [chain_combine(): later[0][:, None, None] * earlier[1] + later[1]]
    dynamic_update_slice x0 -> x4, local copies, waits for them, and re-layouts: none -> 13.9 us  [hold_spans_in(): lax.dynamic_update_slice_in_dim(mat_out, outer, (formed ^ d) * small, axi...]
    all_to_all x1, waiting for transfers between devices: 3.97 us -> 17.6 us  [on_device(): lax.all_to_all(outgoing_pairs, 'head', split_axis=1, concat_axis=0, tiled...]
    all_to_all x1 -> x0, waiting for transfers between devices: 11 us -> none  [on_device(): lax.all_to_all(outgoing_inner, 'head', split_axis=1, concat_axis=0, tiled...]
    convert_element_type x2, other arithmetic: 1.69 us -> 10.7 us  [convolve(): return jax.nn.silu(summed).astype(jnp.bfloat16)]
    all_gather x1, waiting for transfers between devices: 177 us -> 186 us  [prefix(): gathered = jax.tree.map(lambda a: lax.all_gather(a, axis), part)]
  transfers between devices with their start and end apart: 4 -> 6, of which waited for: 3 -> 2; matrix products, arithmetic and copies ran while one was open for 5% -> 6% of each run, Pallas kernels for 0% -> 0%
where the time goes in v1:
time: 509 us; the launch traced here: 506 us
  waiting for transfers between devices  203 us (40%)
  other arithmetic  120 us (24%)
  local copies, waits for them, and re-layouts  95.5 us (19%)
  blocking collectives  55 us (11%)
  between operations  13.9 us (3%)
  starting transfers between devices  11.6 us (2%)
  matrix products  6.4 us (1%)
    all_gather x1, waiting for transfers between devices, prefix(): gathered = jax.tree.map(lambda a: lax.all_gather(a, axis), part)  186 us
    add x31, other arithmetic, chain_combine(): later[0][:, None, None] * earlier[1] + later[1]  99.1 us
    dynamic_slice x62, local copies, waits for them, and re-layouts, one(): lax.dynamic_index_in_dim(a, lap, 0, False)  58.8 us
    all_gather x1, blocking collectives, prefix(): gathered = jax.tree.map(lambda a: lax.all_gather(a, axis), part)  36.2 us
    all_to_all x1, blocking collectives, on_device(): lax.all_to_all(head_rows, 'head', split_axis=0, concat_axis=1, tiled=True)  18.8 us
    all_to_all x1, waiting for transfers between devices, on_device(): lax.all_to_all(outgoing_pairs, 'head', split_axis=1, concat_axis=0, tiled...  17.6 us
    dynamic_update_slice x4, local copies, waits for them, and re-layouts, hold_spans_in(): lax.dynamic_update_slice_in_dim(mat_out, outer, (formed ^ d) * small, axi...  13.9 us
    convert_element_type x2, other arithmetic, convolve(): return jax.nn.silu(summed).astype(jnp.bfloat16)  10.7 us
  transfers between devices with their start and end apart: 6, of which 2 were waited for; matrix products, arithmetic and copies ran while one was open for 6% of the time, Pallas kernels for 0%

profile of v1, /device:TPU:230, one launch (start us, length us, event | category | flops | bytes accessed | tf_op | source)
XLA Modules:
  0.0 506.1 jit_solution(387901333851609167)
XLA Ops:
  9.0 3.5 collective-permute-start
  12.5 2.6 fusion.45
  23.6 1.8 copy.78
  25.5 2.6 maximum_convert_fusion
  28.2 10.4 %multiply_convert_fusion.2 = bf16[64,8192]{0,1:T(8,128)(2,1)S(1)} fusion(f32[68,8192]{0,1:T(8,128)S(1)} %maximum_convert_fusion, f32[8192]{0:T(1024)S(1)} %bitcast.111, f32[8192]{0:T(1024)S(1)} %bitcast.112, f32[8192]{0:T(1024)S(1)} %bitcast.109, f32[8192]{0:T(1024)S(1)} %bitcast.110, f32[8192]{0:T(1024)S(1)} %bitcast.108), kind=kLoop, calls=%fused_computation.18 | loop fusion | flops 6815744 | bytes 9601024 | tf_op jit(solution)/shard_map/convert_element_type | solution.py:35
  46.4 3.4 all-to-all-start
  51.3 2.4 dynamic_update_slice.32
  53.7 17.6 %all-to-all-done = bf16[64,4,512]{2,0,1:T(8,128)(2,1)S(1)} async-done(((bf16[64,4,512]{2,0,1:T(8,128)(2,1)}), bf16[64,4,512]{2,0,1:T(8,128)(2,1)S(1)}, u32[]{:S(2)}, u32[]{:S(2)}) %all-to-all-start) | async-done | bytes 262176 | tf_op jit(solution)/shard_map/all_to_all | solution.py:161
  71.7 5.9 %dynamic_update_slice.33 = bf16[256,2048]{0,1:T(8,128)(2,1)S(1)} dynamic-update-slice(bf16[256,2048]{0,1:T(8,128)(2,1)S(1)} %dynamic_update_slice.32, bf16[64,2048]{0,1:T(8,128)(2,1)} %collective-permute-done.1, s32[]{:T(128)S(6)} %select_n.44, s32[]{:T(128)} %constant.105.clone.1) | dynamic-update-slice | bytes 524292 | tf_op jit(solution)/shard_map/dynamic_update_slice | solution.py:154
  77.7 2.0 dynamic_update_slice.34
  79.7 3.6 dynamic_update_slice.35
  86.8 36.2 %all-gather = f32[32,1,32]{2,1,0:T(1,128)S(1)} all-gather(f32[1,1,32]{2,1,0:T(1,128)S(1)} %copy-done.20), channel_id=2, replica_groups=mesh['rollout'=2,'context'=32,'head'=4] {'context'}, dimensions={0}, use_global_device_ids=true | all-gather | bytes 4224 | tf_op jit(solution)/shard_map/all_gather | solution.py:17
  123.3 4.2 fusion
  127.5 185.5 %all-gather.3.cloned.1.call-done = f32[32,32,128,64]{2,3,1,0:T(8,128)} async-done(((f32[1,32,128,64]{2,3,1,0:T(8,128)}), f32[32,32,128,64]{2,3,1,0:T(8,128)}) %all-gather.3.cloned.1.call-update) | async-done | bytes 33554448 | tf_op jit(solution)/shard_map/all_gather | solution.py:17
  314.6 158.9 %while.3 = (s32[]{:T(128)}, f32[32,128,64]{2,1,0:T(8,128)}, s32[]{:T(128)}, f32[32,32]{1,0:T(8,128)S(1)}, f32[32,32,128,64]{2,3,1,0:T(8,128)}, /*index=5*/s32[]{:T(128)}, s32[]{:T(128)}, s32[]{:T(128)}) while((s32[]{:T(128)}, f32[32,128,64]{2,1,0:T(8,128)}, s32[]{:T(128)}, f32[32,32]{1,0:T(8,128)S(1)}, f32[32,32,128,64]{2,3,1,0:T(8,128)}, ...), condition=%wide.region_1.2_spmd, body=%wide.region_0.1_spmd.sunk | while | flops 524293 | bytes 7340543 | solution.py:25
  316.5 3.2 bitcast_add_fusion.3
  321.6 3.2 bitcast_add_fusion.3
  326.8 3.2 bitcast_add_fusion.3
  331.9 3.2 bitcast_add_fusion.3
  337.0 3.2 bitcast_add_fusion.3
  342.1 3.2 bitcast_add_fusion.3
  347.3 3.2 bitcast_add_fusion.3
  352.4 3.2 bitcast_add_fusion.3
  357.5 3.2 bitcast_add_fusion.3
  362.6 3.2 bitcast_add_fusion.3
  367.8 3.2 bitcast_add_fusion.3
  372.9 3.2 bitcast_add_fusion.3
  378.0 3.2 bitcast_add_fusion.3
  383.1 3.2 bitcast_add_fusion.3
  388.3 3.2 bitcast_add_fusion.3
  393.4 3.2 bitcast_add_fusion.3
  398.5 3.2 bitcast_add_fusion.3
  403.6 3.2 bitcast_add_fusion.3
  408.8 3.2 bitcast_add_fusion.3
  413.9 3.2 bitcast_add_fusion.3
  419.0 3.2 bitcast_add_fusion.3
  424.1 3.2 bitcast_add_fusion.3
  429.3 3.2 bitcast_add_fusion.3
  434.4 3.2 bitcast_add_fusion.3
  439.5 3.2 bitcast_add_fusion.3
  444.6 3.2 bitcast_add_fusion.3
  449.8 3.2 bitcast_add_fusion.3
  454.9 3.2 bitcast_add_fusion.3
  460.0 3.2 bitcast_add_fusion.3
  465.1 3.2 bitcast_add_fusion.3
  470.3 3.2 bitcast_add_fusion.3
  473.5 1.9 convert_element_type.54
  479.4 18.8 %all_to_all.35 = bf16[4,64,2048]{2,1,0:T(8,128)(2,1)S(1)} all-to-all(bf16[4,64,2048]{2,1,0:T(8,128)(2,1)S(1)} %bitcast.102), channel_id=1, replica_groups=mesh['rollout'=2,'context'=32,'head'=4] {'head'}, dimensions={0} | all-to-all | bytes 2097152 | tf_op jit(solution)/shard_map/all_to_all | solution.py:220
  (184 shorter events, 90.1 us)
Async XLA Ops:
  6.5 13.9 %copy-start.4 = (bf16[64,8192]{1,0:T(8,128)(2,1)S(1)}, bf16[64,8192]{1,0:T(8,128)(2,1)}, u32[]{:S(2)}) copy-start(bf16[64,8192]{1,0:T(8,128)(2,1)} %param.12) | copy-start | bytes 3145732
  9.0 13.7 %collective-permute-start = (bf16[4,10240]{1,0:T(4,128)(2,1)}, bf16[4,10240]{1,0:T(4,128)(2,1)}, u32[]{:S(2)}, u32[]{:S(2)}) collective-permute-start(bf16[4,10240]{1,0:T(4,128)(2,1)} %pad_maximum_fusion), channel_id=1, source_target_pairs={{0,1},{1,2},{2,3},{3,4},{4,5},{5,6},{6,7},{7,8},{8,9},{9,10},{10,1... | collective-permute-start | bytes 245768 | tf_op jit(solution)/shard_map/ppermute | solution.py:12
  17.6 2.9 copy-start.16
  17.7 2.8 copy-start.6
  25.4 2.7 copy-start.7
  25.4 2.7 copy-start.8
  25.5 2.7 copy-start.9
  25.5 2.7 copy-start.10
  25.5 2.7 copy-start.11
  38.5 6.7 %copy-start.13 = (f32[1,8,2,128]{3,2,1,0:T(2,128)S(1)}, f32[1,8,2,128]{3,2,1,0:T(2,128)}, u32[]{:S(2)}) copy-start(f32[1,8,2,128]{3,2,1,0:T(2,128)} %get-tuple-element.167) | copy-start | bytes 24580
  38.5 6.7 %copy-start.14 = (f32[1,8,2,128]{3,2,1,0:T(2,128)S(1)}, f32[1,8,2,128]{3,2,1,0:T(2,128)}, u32[]{:S(2)}) copy-start(f32[1,8,2,128]{3,2,1,0:T(2,128)} %get-tuple-element.168) | copy-start | bytes 24580
  38.6 6.7 %copy-start.15 = (f32[1,8,2,128]{3,2,1,0:T(2,128)S(1)}, f32[1,8,2,128]{3,2,1,0:T(2,128)}, u32[]{:S(2)}) copy-start(f32[1,8,2,128]{3,2,1,0:T(2,128)} %get-tuple-element.169) | copy-start | bytes 24580
  39.8 31.9 %collective-permute-start.1 = (bf16[64,2048]{0,1:T(8,128)(2,1)}, bf16[64,2048]{0,1:T(8,128)(2,1)}, u32[]{:S(2)}, u32[]{:S(2)}) collective-permute-start(bf16[64,2048]{0,1:T(8,128)(2,1)} %get-tuple-element.151), channel_id=1, source_target_pairs={{0,1},{1,0},{2,3},{3,2},{4,5},{5,4},{6,7},{7,6},{8,9},{9,8},{10,11... | collective-permute-start | bytes 786440 | tf_op jit(solution)/shard_map/ppermute | solution.py:153
  41.3 36.3 %collective-permute-start.2 = (bf16[64,2048]{0,1:T(8,128)(2,1)}, bf16[64,2048]{0,1:T(8,128)(2,1)S(1)}, u32[]{:S(2)}, u32[]{:S(2)}) collective-permute-start(bf16[64,2048]{0,1:T(8,128)(2,1)} %get-tuple-element.150), channel_id=1, source_target_pairs={{0,2},{1,3},{2,0},{3,1},{4,6},{5,7},{6,4},{7,5},{8,10},{9,11},{10,... | collective-permute-start | bytes 786440 | tf_op jit(solution)/shard_map/ppermute | solution.py:153
  42.7 37.0 %collective-permute-start.3 = (bf16[64,2048]{0,1:T(8,128)(2,1)}, bf16[64,2048]{0,1:T(8,128)(2,1)S(1)}, u32[]{:S(2)}, u32[]{:S(2)}) collective-permute-start(bf16[64,2048]{0,1:T(8,128)(2,1)} %get-tuple-element.149), channel_id=1, source_target_pairs={{0,3},{1,2},{2,1},{3,0},{4,7},{5,6},{6,5},{7,4},{8,11},{9,10},{10,... | collective-permute-start | bytes 786440 | tf_op jit(solution)/shard_map/ppermute | solution.py:153
  46.4 24.8 %all-to-all-start = ((bf16[64,4,512]{2,0,1:T(8,128)(2,1)}), bf16[64,4,512]{2,0,1:T(8,128)(2,1)S(1)}, u32[]{:S(2)}, u32[]{:S(2)}) async-start(bf16[64,4,512]{2,0,1:T(8,128)(2,1)} %bitcast.94), calls=%async_computation | async-start | bytes 524288 | tf_op jit(solution)/shard_map/all_to_all | solution.py:161
  49.8 263.2 %all-gather.3.cloned.1.call-start = ((), (), s32[]{:S(2)}) async-start(), calls=%async_computation.2 | async-start | bytes 34603008 | tf_op jit(solution)/shard_map/all_gather | solution.py:17
  71.3 12.0 %copy-start.12 = (f32[256,32]{0,1:T(8,128)S(1)}, f32[256,32]{0,1:T(8,128)}, u32[]{:S(2)}) copy-start(f32[256,32]{0,1:T(8,128)} %copy.86) | copy-start | bytes 98308
  83.3 40.0 %copy-start = (bf16[256,2048]{0,1:T(8,128)(2,1)}, bf16[256,2048]{0,1:T(8,128)(2,1)S(1)}, u32[]{:S(2)}) copy-start(bf16[256,2048]{0,1:T(8,128)(2,1)S(1)} %dynamic_update_slice.35) | copy-start | bytes 3145732
  83.8 1.6 copy-start.5
  84.9 1.8 copy-start.19
  84.9 1.9 copy-start.20
  84.9 38.4 %copy-start.17 = (f32[32,256]{1,0:T(8,128)S(1)}, f32[32,256]{1,0:T(8,128)}, u32[]{:S(2)}) copy-start(f32[32,256]{1,0:T(8,128)} %copy-done.16) | copy-start | bytes 98308
  473.5 2.5 copy-start.3
  475.4 1.3 copy-start.1
  475.4 1.6 copy-start.2
  477.0 1.4 copy-start.18
Sparse Core Ops, SparseCore 0:
  85.0 227.9 all-gather.2
